TPU v7x, 256 devices: a whole 4x4x8 slice. The times are simulated.
256 devices in a mesh: dp: 32 (over y, z_lo, core), cent: 8 (over x, z_hi).
Axes of the slice: x: 4, y: 4, z: 8 (z_hi: 2, z_lo: 4; z = z_hi * 4 + z_lo), core: 2. Of those that a mesh axis runs over, the one named last changes fastest.
Arguments:
- hidden: bfloat16 [5632, 11008], P('dp', 'cent'), may hold values from -6 to 6
- residual: bfloat16 [5632, 4096], P('dp', 'cent'), may hold values from -6 to 6
- down_weight: bfloat16 [11008, 4096], P('cent', 'dp'), may hold values from -0.0546875 to 0.0546875
- gain: float32 [4096], P('cent'), may hold values from 0.1 to 1.9
- proj_weight: bfloat16 [4096, 1024], P('cent'), may hold values from -0.09375 to 0.09375
- centroids: bfloat16 [131072, 1024], P(('dp', 'cent')), may hold values from -24 to 24
Outputs:
- weighted: float32 [131072, 1024], P(('dp', 'cent'))
- counts: float32 [131072], P(('dp', 'cent'))
All inputs are finite; a program needn't handle non-finite values.
Results may differ from a plain program's by a relative error of at most 0.011.
Values may be sent and summed in bfloat16 or wider, within the bound.
A program may use at most 128 MiB of HBM per device.

v0:
```python
import math
import jax
import jax.numpy as jnp
from jax import lax
from jax.sharding import PartitionSpec as P


def body(hidden, residual, down_weight, gain, proj_weight, centroids):
    partial_layer = jnp.dot(
        hidden,
        lax.all_gather(down_weight, "dp", axis=1, tiled=True),
        preferred_element_type=jnp.float32,
    )
    layer_out = lax.psum_scatter(partial_layer, "cent", scatter_dimension=1, tiled=True)
    normed = ((layer_out + residual.astype(jnp.float32)) * gain).astype(jnp.bfloat16)
    partial_embed = jnp.dot(normed, proj_weight, preferred_element_type=jnp.float32)
    embed_width = proj_weight.shape[1]
    embed_full = lax.psum(partial_embed, "cent")
    scaled = (
        embed_full * lax.rsqrt(jnp.mean(embed_full * embed_full, axis=1, keepdims=True) + 1e-06)
    ).astype(jnp.bfloat16)
    gathered = lax.all_gather(scaled, "dp", axis=0, tiled=True)
    inverse = 1.0 / (math.sqrt(embed_width) * 0.05)
    scores = (
        lax.dot_general(
            gathered, centroids, (((1,), (1,)), ((), ())), preferred_element_type=jnp.float32
        )
        * inverse
    )
    local_max = jnp.max(scores, axis=1)
    row_max = lax.pmax(local_max, ("dp", "cent"))
    row_total = lax.psum(jnp.sum(jnp.exp(scores - row_max[:, None]), axis=1), ("dp", "cent"))
    log_total = row_max + jnp.log(row_total)
    probability = jnp.exp(scores - log_total[:, None])
    scale_up = centroids.shape[0] * lax.axis_size("dp") * lax.axis_size("cent") / gathered.shape[0]
    counts = scale_up * jnp.sum(probability, axis=0)
    prob_low = probability.astype(jnp.bfloat16)
    weighted = scale_up * lax.dot_general(
        prob_low, gathered, (((0,), (0,)), ((), ())), preferred_element_type=jnp.float32
    )
    return (weighted, counts)


def solution(mesh):
    in_specs = (
        P("dp", "cent"),
        P("dp", "cent"),
        P("cent", "dp"),
        P("cent"),
        P("cent", None),
        P(("dp", "cent"), None),
    )
    out_specs = (P(("dp", "cent"), None), P(("dp", "cent")))
    return jax.shard_map(body, mesh=mesh, in_specs=in_specs, out_specs=out_specs, check_vma=False)
```

profile of v0, /device:TPU:1, one launch (start us, length us, event | category | flops | bytes accessed | tf_op | source)
XLA Modules:
  0.0 617.1 jit_solution(13492038344672853306)
XLA Ops:
  7.2 0.0 copy-start
  7.2 0.0 all-gather.3.cloned.1.call-start
  7.3 0.7 all-gather.3.cloned.1.call-update
  7.9 0.0 reduce-scatter.2.cloned.1.call-start
  8.0 105.2 %all-gather.3.cloned.1.call-done = bf16[1376,4096]{1,0:T(8,128)(2,1)} async-done(((bf16[1376,128]{1,0:T(8,128)(2,1)}), bf16[1376,4096]{1,0:T(8,128)(2,1)}) %all-gather.3.cloned.1.call-update) | async-done | bytes 11272208 | tf_op jit(solution)/shard_map/all_gather | solution.py:11
  113.2 8.5 %fusion.11 = f32[176,4096]{1,0:T(8,128)} fusion(bf16[176,1376]{1,0:T(8,128)(2,1)} %param.6, bf16[1376,4096]{1,0:T(8,128)(2,1)} %all-gather.3.cloned.1.call-done), kind=kOutput, calls=%fused_computation.17 | convolution fusion | flops 1983905792 | bytes 14640128 | tf_op jit(solution)/shard_map/dot_general | solution.py:9
  121.7 0.0 reduce-scatter.2.cloned.1.call-update
  121.7 0.0 all-reduce.2.cloned.1.call-start
  121.8 103.8 %reduce-scatter.2.cloned.1.call-done = f32[176,512]{1,0:T(8,128)} async-done(((f32[176,4096]{1,0:T(8,128)}), f32[176,512]{1,0:T(8,128)}) %reduce-scatter.2.cloned.1.call-update) | async-done | bytes 360464 | tf_op jit(solution)/shard_map/reduce_scatter | solution.py:14
  225.6 2.2 fusion.8
  227.8 0.0 all-reduce.2.cloned.1.call-update
  227.8 0.0 all-gather.5.cloned.1.call-start
  227.8 112.2 %all-reduce.2.cloned.1.call-done = f32[176,1024]{1,0:T(8,128)} async-done(((f32[176,1024]{1,0:T(8,128)}), f32[176,1024]{1,0:T(8,128)}) %all-reduce.2.cloned.1.call-update) | async-done | bytes 720912 | tf_op jit(solution)/shard_map/psum | solution.py:18
  340.1 1.2 multiply_reduce_fusion
  341.3 2.0 multiply_convert_fusion
  343.3 0.0 all-gather.5.cloned.1.call-update
  343.3 78.9 %all-gather.5.cloned.1.call-done = bf16[5632,1024]{1,0:T(8,128)(2,1)} async-done(((bf16[176,1024]{1,0:T(8,128)(2,1)}), bf16[5632,1024]{1,0:T(8,128)(2,1)}) %all-gather.5.cloned.1.call-update) | async-done | bytes 11534352 | tf_op jit(solution)/shard_map/all_gather | solution.py:22
  422.2 13.2 %fusion.10 = (f32[5632]{0:T(1024)S(1)}, f32[5632,512]{0,1:T(8,128)}) fusion(bf16[5632,1024]{1,0:T(8,128)(2,1)} %all-gather.5.cloned.1.call-done, bf16[512,1024]{1,0:T(8,128)(2,1)S(1)} %copy-done), kind=kOutput, calls=%fused_computation.16 | convolution fusion | flops 5911341568 | bytes 24139776 | tf_op jit(solution)/shard_map/dot_general | solution.py:25
  435.3 76.1 %pmax.7 = f32[5632]{0:T(1024)S(1)} all-reduce(f32[5632]{0:T(1024)S(1)} %get-tuple-element.2), channel_id=1, replica_groups=mesh['dp'=32,'cent'=8] {'dp','cent'}, use_global_device_ids=true, to_apply=%region_4.0 | all-reduce | flops 5632 | bytes 45056 | tf_op jit(solution)/shard_map/pmax | solution.py:31
  511.4 6.0 exponential_reduce_fusion
  517.4 73.3 %psum.15 = f32[5632]{0:T(1024)S(1)} all-reduce(f32[5632]{0:T(1024)S(1)} %exponential_reduce_fusion), channel_id=1, replica_groups=mesh['dp'=32,'cent'=8] {'dp','cent'}, use_global_device_ids=true, to_apply=%region_6.0 | all-reduce | flops 5632 | bytes 45056 | tf_op jit(solution)/shard_map/psum | solution.py:32
  590.7 6.0 fusion
  596.7 0.6 broadcast_multiply_fusion
  597.3 13.3 %fusion.5 = f32[512,1024]{1,0:T(8,128)} fusion(bf16[5632,1024]{1,0:T(8,128)(2,1)} %all-gather.5.cloned.1.call-done, f32[5632,512]{0,1:T(8,128)} %get-tuple-element.3, f32[5632]{0:T(1024)S(1)} %log_add_fusion), kind=kOutput, calls=%fused_computation.7 | convolution fusion | flops 5911871488 | bytes 25188352 | tf_op jit(solution)/shard_map/dot_general | solution.py:38
  (9 shorter events, 0.0 us)
Async XLA Ops:
  7.2 415.0 %copy-start = (bf16[512,1024]{1,0:T(8,128)(2,1)S(1)}, bf16[512,1024]{1,0:T(8,128)(2,1)}, u32[]{:S(2)}) copy-start(bf16[512,1024]{1,0:T(8,128)(2,1)} %param.11) | copy-start | bytes 3145732
  7.2 218.4 %copy-start.1 = (bf16[512,1024]{1,0:T(8,128)(2,1)S(1)}, bf16[512,1024]{1,0:T(8,128)(2,1)}, u32[]{:S(2)}) copy-start(bf16[512,1024]{1,0:T(8,128)(2,1)} %param.10) | copy-start | bytes 3145732
  7.2 218.4 %copy-start.3 = (f32[512]{0:T(512)S(1)}, f32[512]{0:T(512)}, u32[]{:S(2)}) copy-start(f32[512]{0:T(512)} %param.9) | copy-start | bytes 6148
  7.2 218.4 %copy-start.2 = (bf16[176,512]{1,0:T(8,128)(2,1)S(1)}, bf16[176,512]{1,0:T(8,128)(2,1)}, u32[]{:S(2)}) copy-start(bf16[176,512]{1,0:T(8,128)(2,1)} %param.7) | copy-start | bytes 540676
  7.2 106.0 %all-gather.3.cloned.1.call-start = ((), (), s32[]{:S(2)}) async-start(), calls=%async_computation.1 | async-start | bytes 11624448 | tf_op jit(solution)/shard_map/all_gather | solution.py:11
  7.9 217.6 %reduce-scatter.2.cloned.1.call-start = ((), (), s32[]{:S(2)}) async-start(), calls=%async_computation.2 | async-start | bytes 3244032 | tf_op jit(solution)/shard_map/reduce_scatter | solution.py:14
  121.7 218.3 %all-reduce.2.cloned.1.call-start = ((), (), s32[]{:S(2)}) async-start(), calls=%async_computation.3 | async-start | bytes 1441792 | tf_op jit(solution)/shard_map/psum | solution.py:18
  227.8 194.4 %all-gather.5.cloned.1.call-start = ((), (), s32[]{:S(2)}) async-start(), calls=%async_computation.4 | async-start | bytes 11894784 | tf_op jit(solution)/shard_map/all_gather | solution.py:22
Sparse Core Ops, SparseCore 0:
  9.8 103.3 all-gather.2
  121.8 103.6 reduce-scatter.1
  228.8 111.2 all-reduce.1
  343.4 78.7 all-gather.4
where the time goes:
time: 618 us; the launch traced here: 617 us
  waiting for transfers between devices  401 us (65%)
  blocking collectives  149 us (24%)
  matrix products  37.1 us (6%)
  other arithmetic  15.8 us (3%)
  between operations  13.8 us (2%)
    psum x1, waiting for transfers between devices, body(): embed_full = lax.psum(partial_embed, 'cent')  112 us
    all_gather x1, waiting for transfers between devices, body(): lax.all_gather(down_weight, 'dp', axis=1, tiled=True)  105 us
    reduce_scatter x1, waiting for transfers between devices, body(): lax.psum_scatter(partial_layer, 'cent', scatter_dimension=1, tiled=True)  104 us
    all_gather x1, waiting for transfers between devices, body(): gathered = lax.all_gather(scaled, 'dp', axis=0, tiled=True)  78.9 us
    pmax x1, blocking collectives, body(): row_max = lax.pmax(local_max, ('dp', 'cent'))  76.1 us
    psum x1, blocking collectives, body(): lax.psum(jnp.sum(jnp.exp(scores - row_max[:, None]), axis=1), ('dp', 'cen...  73.3 us
    dot_general x1, matrix products, body(): lax.dot_general(prob_low, gathered, (((0,), (0,)), ((), ())), preferred_e...  13.3 us
    dot_general x1, matrix products, body(): lax.dot_general(gathered, centroids, (((1,), (1,)), ((), ())), preferred_...  13.2 us
  transfers between devices with their start and end apart: 4, of which 4 were waited for; matrix products, arithmetic and copies ran while one was open for 0% of the time, Pallas kernels for 0%

commit v1 on v0

--- a/solution.py
+++ b/solution.py
@@ -29,7 +29,9 @@
     )
     local_max = jnp.max(scores, axis=1)
     row_max = lax.pmax(local_max, ("dp", "cent"))
-    row_total = lax.psum(jnp.sum(jnp.exp(scores - row_max[:, None]), axis=1), ("dp", "cent"))
+    xx = jnp.sum(jnp.exp(scores - row_max[:, None]), axis=1)
+    oldest = lax.psum(xx, "cent")
+    row_total = lax.psum(oldest, axis_name="dp")
     log_total = row_max + jnp.log(row_total)
     probability = jnp.exp(scores - log_total[:, None])
     scale_up = centroids.shape[0] * lax.axis_size("dp") * lax.axis_size("cent") / gathered.shape[0]

time: 618 us -> 725 us (1.17)
  blocking collectives: 149 us -> 254 us
    psum x1 -> x2, blocking collectives: 73.3 us -> 178 us  [the longest x1 135 us: body(): row_total = lax.psum(oldest, axis_name='dp')]
where the time goes in v1:
time: 725 us; the launch traced here: 722 us
  waiting for transfers between devices  401 us (55%)
  blocking collectives  254 us (35%)
  matrix products  37.1 us (5%)
  other arithmetic  15.8 us (2%)
  between operations  13.8 us (2%)
    psum x1, blocking collectives, body(): row_total = lax.psum(oldest, axis_name='dp')  135 us
    psum x1, waiting for transfers between devices, body(): embed_full = lax.psum(partial_embed, 'cent')  112 us
    all_gather x1, waiting for transfers between devices, body(): lax.all_gather(down_weight, 'dp', axis=1, tiled=True)  105 us
    reduce_scatter x1, waiting for transfers between devices, body(): lax.psum_scatter(partial_layer, 'cent', scatter_dimension=1, tiled=True)  104 us
    all_gather x1, waiting for transfers between devices, body(): gathered = lax.all_gather(scaled, 'dp', axis=0, tiled=True)  78.9 us
    pmax x1, blocking collectives, body(): row_max = lax.pmax(local_max, ('dp', 'cent'))  76.1 us
    psum x1, blocking collectives, body(): oldest = lax.psum(xx, 'cent')  43 us
  transfers between devices with their start and end apart: 4, of which 4 were waited for; matrix products, arithmetic and copies ran while one was open for 0% of the time, Pallas kernels for 0%

profile of v1, /device:TPU:1, one launch (start us, length us, event | category | flops | bytes accessed | tf_op | source)
XLA Modules:
  0.0 721.9 jit_solution(5973930479239009705)
XLA Ops:
  7.2 0.0 all-gather.3.cloned.1.call-start
  7.3 0.7 all-gather.3.cloned.1.call-update
  7.9 0.0 reduce-scatter.2.cloned.1.call-start
  8.0 105.2 %all-gather.3.cloned.1.call-done = bf16[1376,4096]{1,0:T(8,128)(2,1)} async-done(((bf16[1376,128]{1,0:T(8,128)(2,1)}), bf16[1376,4096]{1,0:T(8,128)(2,1)}) %all-gather.3.cloned.1.call-update) | async-done | bytes 11272208 | tf_op jit(solution)/shard_map/all_gather | solution.py:11
  113.2 8.5 %fusion.11 = f32[176,4096]{1,0:T(8,128)} fusion(bf16[176,1376]{1,0:T(8,128)(2,1)} %param.6, bf16[1376,4096]{1,0:T(8,128)(2,1)} %all-gather.3.cloned.1.call-done), kind=kOutput, calls=%fused_computation.17 | convolution fusion | flops 1983905792 | bytes 14640128 | tf_op jit(solution)/shard_map/dot_general | solution.py:9
  121.7 0.0 reduce-scatter.2.cloned.1.call-update
  121.7 0.0 all-reduce.2.cloned.1.call-start
  121.8 103.8 %reduce-scatter.2.cloned.1.call-done = f32[176,512]{1,0:T(8,128)} async-done(((f32[176,4096]{1,0:T(8,128)}), f32[176,512]{1,0:T(8,128)}) %reduce-scatter.2.cloned.1.call-update) | async-done | bytes 360464 | tf_op jit(solution)/shard_map/reduce_scatter | solution.py:14
  225.6 2.2 fusion.8
  227.8 0.0 all-reduce.2.cloned.1.call-update
  227.8 0.0 all-gather.5.cloned.1.call-start
  227.8 112.2 %all-reduce.2.cloned.1.call-done = f32[176,1024]{1,0:T(8,128)} async-done(((f32[176,1024]{1,0:T(8,128)}), f32[176,1024]{1,0:T(8,128)}) %all-reduce.2.cloned.1.call-update) | async-done | bytes 720912 | tf_op jit(solution)/shard_map/psum | solution.py:18
  340.1 1.2 multiply_reduce_fusion
  341.3 2.0 multiply_convert_fusion
  343.3 0.0 all-gather.5.cloned.1.call-update
  343.3 78.9 %all-gather.5.cloned.1.call-done = bf16[5632,1024]{1,0:T(8,128)(2,1)} async-done(((bf16[176,1024]{1,0:T(8,128)(2,1)}), bf16[5632,1024]{1,0:T(8,128)(2,1)}) %all-gather.5.cloned.1.call-update) | async-done | bytes 11534352 | tf_op jit(solution)/shard_map/all_gather | solution.py:22
  422.2 13.2 %fusion.10 = (f32[5632]{0:T(1024)S(1)}, f32[5632,512]{0,1:T(8,128)}) fusion(bf16[5632,1024]{1,0:T(8,128)(2,1)} %all-gather.5.cloned.1.call-done, bf16[512,1024]{1,0:T(8,128)(2,1)S(1)} %copy-done), kind=kOutput, calls=%fused_computation.16 | convolution fusion | flops 5911341568 | bytes 24139776 | tf_op jit(solution)/shard_map/dot_general | solution.py:25
  435.3 76.1 %pmax.7 = f32[5632]{0:T(1024)S(1)} all-reduce(f32[5632]{0:T(1024)S(1)} %get-tuple-element.2), channel_id=1, replica_groups=mesh['dp'=32,'cent'=8] {'dp','cent'}, use_global_device_ids=true, to_apply=%region_4.0 | all-reduce | flops 5632 | bytes 45056 | tf_op jit(solution)/shard_map/pmax | solution.py:31
  511.4 6.0 exponential_reduce_fusion
  517.4 43.0 %psum.22 = f32[5632]{0:T(1024)S(1)} all-reduce(f32[5632]{0:T(1024)S(1)} %exponential_reduce_fusion), channel_id=1, replica_groups=mesh['dp'=32,'cent'=8] {'cent'}, use_global_device_ids=true, to_apply=%region_6.0 | all-reduce | flops 5632 | bytes 45056 | tf_op jit(solution)/shard_map/psum | solution.py:33
  560.4 135.1 %psum.23 = f32[5632]{0:T(1024)S(1)} all-reduce(f32[5632]{0:T(1024)S(1)} %psum.22), channel_id=1, replica_groups=mesh['dp'=32,'cent'=8] {'dp'}, use_global_device_ids=true, to_apply=%region_7.0 | all-reduce | flops 5632 | bytes 45056 | tf_op jit(solution)/shard_map/psum | solution.py:34
  695.5 6.0 fusion
  701.5 0.6 broadcast_multiply_fusion
  702.1 13.3 %fusion.5 = f32[512,1024]{1,0:T(8,128)} fusion(bf16[5632,1024]{1,0:T(8,128)(2,1)} %all-gather.5.cloned.1.call-done, f32[5632,512]{0,1:T(8,128)} %get-tuple-element.3, f32[5632]{0:T(1024)S(1)} %log_add_fusion), kind=kOutput, calls=%fused_computation.7 | convolution fusion | flops 5911871488 | bytes 25188352 | tf_op jit(solution)/shard_map/dot_general | solution.py:40
  (10 shorter events, 0.0 us)
Async XLA Ops:
  7.2 415.0 %copy-start = (bf16[512,1024]{1,0:T(8,128)(2,1)S(1)}, bf16[512,1024]{1,0:T(8,128)(2,1)}, u32[]{:S(2)}) copy-start(bf16[512,1024]{1,0:T(8,128)(2,1)} %param.11) | copy-start | bytes 3145732
  7.2 218.4 %copy-start.1 = (bf16[512,1024]{1,0:T(8,128)(2,1)S(1)}, bf16[512,1024]{1,0:T(8,128)(2,1)}, u32[]{:S(2)}) copy-start(bf16[512,1024]{1,0:T(8,128)(2,1)} %param.10) | copy-start | bytes 3145732
  7.2 218.4 %copy-start.3 = (f32[512]{0:T(512)S(1)}, f32[512]{0:T(512)}, u32[]{:S(2)}) copy-start(f32[512]{0:T(512)} %param.9) | copy-start | bytes 6148
  7.2 218.4 %copy-start.2 = (bf16[176,512]{1,0:T(8,128)(2,1)S(1)}, bf16[176,512]{1,0:T(8,128)(2,1)}, u32[]{:S(2)}) copy-start(bf16[176,512]{1,0:T(8,128)(2,1)} %param.7) | copy-start | bytes 540676
  7.2 106.0 %all-gather.3.cloned.1.call-start = ((), (), s32[]{:S(2)}) async-start(), calls=%async_computation.1 | async-start | bytes 11624448 | tf_op jit(solution)/shard_map/all_gather | solution.py:11
  7.9 217.6 %reduce-scatter.2.cloned.1.call-start = ((), (), s32[]{:S(2)}) async-start(), calls=%async_computation.2 | async-start | bytes 3244032 | tf_op jit(solution)/shard_map/reduce_scatter | solution.py:14
  121.7 218.3 %all-reduce.2.cloned.1.call-start = ((), (), s32[]{:S(2)}) async-start(), calls=%async_computation.3 | async-start | bytes 1441792 | tf_op jit(solution)/shard_map/psum | solution.py:18
  227.8 194.4 %all-gather.5.cloned.1.call-start = ((), (), s32[]{:S(2)}) async-start(), calls=%async_computation.4 | async-start | bytes 11894784 | tf_op jit(solution)/shard_map/all_gather | solution.py:22
Sparse Core Ops, SparseCore 0:
  9.8 103.3 all-gather.2
  121.8 103.6 reduce-scatter.1
  228.8 111.2 all-reduce.1
  343.4 78.7 all-gather.4
